TPU v7x, 512 devices: a whole 4x8x8 slice. The times are simulated.
512 devices in a mesh: image: 16 (over z, core), ri: 32 (over y, x).
Axes of the slice: x: 4, y: 8, z: 8, core: 2. Of those that a mesh axis runs over, the one named last changes fastest.
Arguments:
- blocks: bfloat16 [16384, 64, 256], P(('image', 'ri')), may hold values from -2.5 to 2.5
- block_owner: int32 [16384, 1], P(('image', 'ri')), may hold values from 0 to 31; in each aligned block of 32 rows (0 to 31, 32 to 63, ...) at most 2 rows name the same one
- block_basis: int32 [16384, 2], P(('image', 'ri')), may hold values from 0 to 255
- pair_images: int32 [16384, 2, 4], P(('image', 'ri')), may hold values from 0 to 15
- pair_cell: int32 [16384, 4], P(('image', 'ri')), may hold values from 0 to 3
- lattice: int32 [4, 2], replicated, may hold values from -3 to 3
- dens_occ: bfloat16 [16, 256, 64], P('image'), may hold values from -1.5 to 1.5
- dens_virt: bfloat16 [16, 256, 64], P('image'), may hold values from -1.5 to 1.5
Outputs:
- chi_k: float32 [2, 64, 32, 256, 256], P(None, None, 'ri', 'image')
Inputs may be any that keep to these rules, and one draw needn't show every extreme that they name: `block_owner`: within the 32 blocks of one device no owner is named by more than 2 blocks.
All inputs are finite; a program needn't handle non-finite values.
Results may differ from a plain program's by a relative error of at most 0.0041.
Values may be sent and summed in bfloat16 or wider, within the bound.
A program may use at most 128 MiB of HBM per device.

v0:
```python
import math

import jax
import jax.numpy as jnp
from jax import lax
from jax.sharding import PartitionSpec as P

KGRID = 8


def density_terms(occ_piece, first_image, virt_whole, listing, pair_count, cell_count):
    image_count, block_count, square = occ_piece.shape
    side_len = math.isqrt(square)
    row_count = listing.shape[0]
    first_block = listing[:, 0]
    second = listing[:, 1]
    occ_img = listing[:, 2 : 2 + pair_count]
    virt_img = listing[:, 2 + pair_count : 2 + 2 * pair_count]
    cell_ids = listing[:, 2 + 2 * pair_count : 2 + 3 * pair_count]
    offset = occ_img - first_image
    inside = ((offset >= 0) & (offset < image_count)).astype(jnp.float32)
    occ_rows = jnp.clip(offset, 0, image_count - 1) * block_count + first_block[:, None]
    virt_rows = virt_img * block_count + second[:, None]
    occ_vals = (
        occ_piece.reshape(image_count * block_count, square)[occ_rows].astype(jnp.float32)
        * inside[:, :, None]
    )
    virt_vals = virt_whole.reshape(-1, square)[virt_rows].astype(jnp.float32)
    select = (
        cell_ids[:, :, None] == jnp.arange(cell_count, dtype=jnp.int32)[None, None, :]
    ).astype(jnp.float32)
    term_sum = jnp.einsum(
        "sjr,sjlm,sjnq->srlqmn",
        select,
        occ_vals.reshape(row_count, pair_count, side_len, side_len),
        virt_vals.reshape(row_count, pair_count, side_len, side_len),
        precision=lax.Precision.HIGHEST,
    )
    return term_sum.reshape(row_count, cell_count, square, square)


def operators(listing, occ_local, virt_local, pair_count, cell_count):
    occ_whole, virt_whole = (
        lax.all_gather(occ_local, "image", axis=0, tiled=True),
        lax.all_gather(virt_local, "image", axis=0, tiled=True),
    )
    summed = density_terms(occ_whole, 0, virt_whole, listing, pair_count, cell_count)
    return summed.astype(jnp.bfloat16)


def local(blocks, block_owner, block_basis, pair_images, pair_cell, lattice, dens_occ, dens_virt):
    owners = lax.axis_size("ri")
    local_rows, square, ri_width = blocks.shape
    pair_count = pair_cell.shape[1]
    cell_count = lattice.shape[0]
    capacity = max(2, (2 * local_rows + owners - 1) // owners)
    slot_count = owners * capacity
    target = block_owner[:, 0]
    order_ids = jnp.arange(local_rows, dtype=jnp.int32)
    same_owner = (target[:, None] == target[None, :]) & (order_ids[:, None] > order_ids[None, :])
    owner_rank = jnp.sum(same_owner.astype(jnp.int32), axis=1)
    slot_index = target * capacity + owner_rank
    listing = jnp.concatenate(
        [block_basis, pair_images[:, 0, :], pair_images[:, 1, :], pair_cell], axis=1
    )
    packed = jnp.zeros((slot_count, square, ri_width), blocks.dtype).at[slot_index].set(blocks)
    packed_list = jnp.zeros((slot_count, listing.shape[1]), jnp.int32).at[slot_index].set(listing)
    got_blocks, got_list = (
        lax.all_to_all(
            packed.reshape(owners, capacity, square, ri_width),
            "ri",
            split_axis=0,
            concat_axis=0,
            tiled=True,
        ),
        lax.all_to_all(
            packed_list.reshape(owners, capacity, listing.shape[1]),
            "ri",
            split_axis=0,
            concat_axis=0,
            tiled=True,
        ),
    )
    got_blocks = got_blocks.reshape(slot_count, square, ri_width)
    density_ops = operators(
        got_list.reshape(slot_count, listing.shape[1]), dens_occ, dens_virt, pair_count, cell_count
    )
    group_size = 16
    group_count = slot_count // group_size

    def accumulate(running, pieces):
        op_part, blk_part = pieces
        mixed_rows = jnp.einsum(
            "srkm,smp->srkp", op_part, blk_part, preferred_element_type=jnp.float32
        ).astype(jnp.bfloat16)
        return (
            running
            + jnp.einsum("srkp,skq->rpq", mixed_rows, blk_part, preferred_element_type=jnp.float32),
            None,
        )

    start_total = jnp.zeros((cell_count, ri_width, ri_width), jnp.float32)
    chi_cells, _ = lax.scan(
        accumulate,
        start_total,
        (
            density_ops.reshape(group_count, group_size, cell_count, square, square),
            got_blocks.reshape(group_count, group_size, square, ri_width),
        ),
    )
    chi_share = lax.psum_scatter(chi_cells, "image", scatter_dimension=1, tiled=True)
    share_rows = chi_share.shape[1]
    points = jnp.arange(KGRID * KGRID, dtype=jnp.int32)
    wrapped = (
        (points // KGRID)[:, None] * lattice[None, :, 0]
        + (points % KGRID)[:, None] * lattice[None, :, 1]
    ) % KGRID
    angles = 2.0 * math.pi / KGRID * wrapped.astype(jnp.float32)
    phases = jnp.concatenate([jnp.cos(angles), jnp.sin(angles)], axis=0)
    result = jnp.dot(
        phases,
        chi_share.reshape(cell_count, share_rows * ri_width),
        precision=lax.Precision.HIGHEST,
    )
    return result.reshape(2, KGRID * KGRID, 1, share_rows, ri_width)


def solution(mesh):
    placed = (
        P(("image", "ri"), None, None),
        P(("image", "ri"), None),
        P(("image", "ri"), None),
        P(("image", "ri"), None, None),
        P(("image", "ri"), None),
        P(),
        P("image", None, None),
        P("image", None, None),
    )
    return jax.shard_map(
        local,
        mesh=mesh,
        in_specs=placed,
        out_specs=P(None, None, "ri", "image", None),
        check_vma=False,
    )
```

profile of v0, /device:TPU:1, one launch (start us, length us, event | category | flops | bytes accessed | tf_op | source)
XLA Modules:
  0.0 290.1 jit_solution(15780600803534375313)
XLA Ops:
  6.5 0.7 slice_bitcast_fusion.1
  7.2 0.7 pad_add_fusion
  7.9 0.1 copy.59
  8.0 0.9 convert_reduce_fusion
  8.9 0.7 fusion.35
  9.6 1.2 scatter_custom_fusion
  10.8 10.5 %all-to-all-start = ((s32[32,2,14]{2,1,0:T(2,128)}), s32[32,2,14]{2,1,0:T(2,128)S(1)}, u32[]{:S(2)}, u32[]{:S(2)}) async-start(s32[32,2,14]{2,1,0:T(2,128)} %bitcast.9), calls=%async_computation | async-start | bytes 65536 | tf_op jit(solution)/shard_map/all_to_all | solution.py:76
  21.3 1.6 broadcast_in_dim.28
  22.9 0.0 copy-start.2
  22.9 0.0 copy-start.3
  22.9 5.2 %scatter_fusion = bf16[64,64,256]{2,1,0:T(8,128)(2,1)} fusion(bf16[64,64,256]{2,1,0:T(8,128)(2,1)} %broadcast_in_dim.28, s32[32]{0:T(128)S(1)} %fusion.35, bf16[32,64,256]{2,1,0:T(8,128)(2,1)} %param.10), kind=kCustom, calls=%fused_computation.3 | custom fusion | bytes 3145856 | tf_op jit(solution)/shard_map/scatter | solution.py:66
  28.2 1.9 all-to-all-done
  30.0 7.5 %all-to-all-start.1 = ((bf16[32,2,64,256]{3,2,1,0:T(8,128)(2,1)}), bf16[32,2,64,256]{3,2,1,0:T(8,128)(2,1)}, u32[]{:S(2)}, u32[]{:S(2)}) async-start(bf16[32,2,64,256]{3,2,1,0:T(8,128)(2,1)} %bitcast.16), calls=%async_computation.1 | async-start | bytes 4194304 | tf_op jit(solution)/shard_map/all_to_all | solution.py:69
  37.5 0.0 reduce-scatter.2.cloned.1.call-start
  37.6 0.0 copy-done.2
  37.6 25.9 %all_gather.6 = bf16[16,256,64]{1,2,0:T(8,128)(2,1)S(1)} all-gather(bf16[1,256,64]{1,2,0:T(8,128)(2,1)S(1)} %copy-done.2), channel_id=1, replica_groups=mesh['image'=16,'ri'=32] {'image'}, dimensions={0}, use_global_device_ids=true | all-gather | bytes 557056 | tf_op jit(solution)/shard_map/all_gather | solution.py:44
  63.5 0.5 copy.58
  64.0 0.0 copy-done.3
  64.0 15.9 %all_gather.7 = bf16[16,256,64]{1,2,0:T(8,128)(2,1)S(1)} all-gather(bf16[1,256,64]{1,2,0:T(8,128)(2,1)S(1)} %copy-done.3), channel_id=1, replica_groups=mesh['image'=16,'ri'=32] {'image'}, dimensions={0}, use_global_device_ids=true | all-gather | bytes 557056 | tf_op jit(solution)/shard_map/all_gather | solution.py:45
  79.9 0.5 copy.64
  80.4 0.1 fusion.36
  80.5 0.1 copy.80
  80.6 0.1 copy.81
  80.6 0.2 slice_reduce_fusion
  80.9 0.1 copy.61
  81.0 0.1 reshape.76
  81.1 0.9 gather_fusion
  81.9 0.3 reshape.73
  82.3 0.1 copy.62
  82.4 0.3 broadcast_multiply_fusion
  82.7 0.3 copy.63
  83.0 0.1 copy.66
  83.1 0.1 reshape.84
  83.2 0.9 gather_fusion.1
  84.0 0.4 reshape.69
  84.4 33.8 %convert_bitcast_fusion = bf16[64,4,8,8,8,8]{3,4,5,1,2,0:T(8,128)(2,1)} fusion(f32[64,4,4]{1,2,0:T(4,128)S(1)} %fusion.25, f32[64,4,8,8]{3,1,2,0:T(4,128)S(1)} %copy.63, bf16[64,4,8,8,1,1]{3,2,1,0,5,4:T(8,128)(2,1)S(1)} %bitcast.73), kind=kOutput, calls=%fused_computation.14 | convolution fusion | flops 51445760 | bytes 2199552 | tf_op jit(solution)/shard_map/sjr,sjlm,sjnq->srlqmn/dot_general | solution.py:32
  118.2 44.4 %copy.68 = bf16[64,4,8,8,8,8]{0,5,4,3,2,1:T(8,128)(2,1)} copy(bf16[64,4,8,8,8,8]{3,4,5,1,2,0:T(8,128)(2,1)} %convert_bitcast_fusion) | data formatting | bytes 4194304 | tf_op jit(solution)/shard_map/convert_element_type | solution.py:48
  162.7 21.9 %convert_element_type.38 = bf16[4,16,4,64,64]{1,0,4,3,2:T(4,128)(2,1)} reshape(bf16[64,4,8,8,8,8]{0,5,4,3,2,1:T(8,128)(2,1)} %copy.68) | data formatting | bytes 4194304 | tf_op jit(solution)/shard_map/convert_element_type | solution.py:48
  184.6 0.0 copy-start
  184.6 25.3 %copy.69 = bf16[4,16,4,64,64]{4,3,1,2,0:T(8,128)(2,1)} copy(bf16[4,16,4,64,64]{1,0,4,3,2:T(4,128)(2,1)} %convert_element_type.38) | data formatting | bytes 4194304
  209.8 0.0 all-to-all-done.1
  209.8 0.0 copy-done
  209.8 0.0 copy-start.4
  209.8 12.4 %while.11 = (s32[]{:T(128)}, f32[4,256,256]{2,1,0:T(8,128)S(1)}, bf16[4,16,4,64,64]{4,3,1,2,0:T(8,128)(2,1)}, bf16[4,16,64,256]{3,2,1,0:T(8,128)(2,1)}, s32[]{:T(128)}, /*index=5*/s32[]{:T(128)}) while((s32[]{:T(128)}, f32[4,256,256]{2,1,0:T(8,128)S(1)}, bf16[4,16,4,64,64]{4,3,1,2,0:T(8,128)(2,1)}, ...), condition=%wide.region_4.5_spmd.clone, body=%wide.region_3.4_spmd.clone.sunk | while | flops 672661504 | bytes 4195919 | solution.py:103
  209.9 3.1 %fusion.51 = f32[4,256,256]{2,1,0:T(8,128)S(1)} fusion(f32[4,256,256]{2,1,0:T(8,128)S(1)} %get-tuple-element.118, bf16[4,16,4,64,64]{4,3,1,2,0:T(8,128)(2,1)} %get-tuple-element.125, s32[]{:T(128)} %get-tuple-element.117, bf16[4,16,64,256]{3,2,1,0:T(8,128)(2,1)} %get-tuple-element.126, pred[]{:T(512)S(6)} %compare.9), kind=kOutput, calls=%fused_computation.8.clone.1 | convolution fusion | flops 672661504 | bytes 4195841 | tf_op jit(solution)/shard_map/while/body/eval_jaxpr/srkp,skq->rpq/dot_general | solution.py:98
  213.0 3.1 %fusion.51 = f32[4,256,256]{2,1,0:T(8,128)S(1)} fusion(f32[4,256,256]{2,1,0:T(8,128)S(1)} %get-tuple-element.118, bf16[4,16,4,64,64]{4,3,1,2,0:T(8,128)(2,1)} %get-tuple-element.125, s32[]{:T(128)} %get-tuple-element.117, bf16[4,16,64,256]{3,2,1,0:T(8,128)(2,1)} %get-tuple-element.126, pred[]{:T(512)S(6)} %compare.9), kind=kOutput, calls=%fused_computation.8.clone.1 | convolution fusion | flops 672661504 | bytes 4195841 | tf_op jit(solution)/shard_map/while/body/eval_jaxpr/srkp,skq->rpq/dot_general | solution.py:98
  216.1 3.1 %fusion.51 = f32[4,256,256]{2,1,0:T(8,128)S(1)} fusion(f32[4,256,256]{2,1,0:T(8,128)S(1)} %get-tuple-element.118, bf16[4,16,4,64,64]{4,3,1,2,0:T(8,128)(2,1)} %get-tuple-element.125, s32[]{:T(128)} %get-tuple-element.117, bf16[4,16,64,256]{3,2,1,0:T(8,128)(2,1)} %get-tuple-element.126, pred[]{:T(512)S(6)} %compare.9), kind=kOutput, calls=%fused_computation.8.clone.1 | convolution fusion | flops 672661504 | bytes 4195841 | tf_op jit(solution)/shard_map/while/body/eval_jaxpr/srkp,skq->rpq/dot_general | solution.py:98
  219.2 3.1 %fusion.51 = f32[4,256,256]{2,1,0:T(8,128)S(1)} fusion(f32[4,256,256]{2,1,0:T(8,128)S(1)} %get-tuple-element.118, bf16[4,16,4,64,64]{4,3,1,2,0:T(8,128)(2,1)} %get-tuple-element.125, s32[]{:T(128)} %get-tuple-element.117, bf16[4,16,64,256]{3,2,1,0:T(8,128)(2,1)} %get-tuple-element.126, pred[]{:T(512)S(6)} %compare.9), kind=kOutput, calls=%fused_computation.8.clone.1 | convolution fusion | flops 672661504 | bytes 4195841 | tf_op jit(solution)/shard_map/while/body/eval_jaxpr/srkp,skq->rpq/dot_general | solution.py:98
  222.3 0.0 copy-start.1
  222.3 1.0 copy-done.1
  223.2 0.0 reduce-scatter.2.cloned.1.call-update
  223.3 0.0 copy-done.4
  223.3 0.1 fusion.34
  223.4 0.1 pad_maximum_fusion
  223.5 0.1 dot_general.25
  223.6 54.4 %reduce-scatter.2.cloned.1.call-done = f32[4,16,256]{2,1,0:T(8,128)} async-done(((f32[4,256,256]{2,1,0:T(8,128)}), f32[4,16,256]{2,1,0:T(8,128)}) %reduce-scatter.2.cloned.1.call-update) | async-done | bytes 65552 | tf_op jit(solution)/shard_map/reduce_scatter | solution.py:111
  278.0 2.7 convolution_bitcast_fusion
  280.7 2.5 copy.71
  (8 shorter events, 0.1 us)
Async XLA Ops:
  10.8 19.2 %all-to-all-start = ((s32[32,2,14]{2,1,0:T(2,128)}), s32[32,2,14]{2,1,0:T(2,128)S(1)}, u32[]{:S(2)}, u32[]{:S(2)}) async-start(s32[32,2,14]{2,1,0:T(2,128)} %bitcast.9), calls=%async_computation | async-start | bytes 65536 | tf_op jit(solution)/shard_map/all_to_all | solution.py:76
  22.9 14.7 %copy-start.2 = (bf16[1,256,64]{1,2,0:T(8,128)(2,1)S(1)}, bf16[1,256,64]{1,2,0:T(8,128)(2,1)}, u32[]{:S(2)}) copy-start(bf16[1,256,64]{1,2,0:T(8,128)(2,1)} %param.16) | copy-start | bytes 98308
  22.9 41.1 %copy-start.3 = (bf16[1,256,64]{1,2,0:T(8,128)(2,1)S(1)}, bf16[1,256,64]{1,2,0:T(8,128)(2,1)}, u32[]{:S(2)}) copy-start(bf16[1,256,64]{1,2,0:T(8,128)(2,1)} %param.17) | copy-start | bytes 98308
  30.0 179.8 %all-to-all-start.1 = ((bf16[32,2,64,256]{3,2,1,0:T(8,128)(2,1)}), bf16[32,2,64,256]{3,2,1,0:T(8,128)(2,1)}, u32[]{:S(2)}, u32[]{:S(2)}) async-start(bf16[32,2,64,256]{3,2,1,0:T(8,128)(2,1)} %bitcast.16), calls=%async_computation.1 | async-start | bytes 4194304 | tf_op jit(solution)/shard_map/all_to_all | solution.py:69
  37.5 240.5 %reduce-scatter.2.cloned.1.call-start = ((), (), s32[]{:S(2)}) async-start(), calls=%async_computation.3 | async-start | bytes 1114112 | tf_op jit(solution)/shard_map/reduce_scatter | solution.py:111
  184.6 25.3 %copy-start = (f32[4,256,256]{2,1,0:T(8,128)S(1)}, f32[4,256,256]{2,1,0:T(8,128)}, u32[]{:S(2)}) copy-start(f32[4,256,256]{2,1,0:T(8,128)} %custom-call) | copy-start | bytes 3145732
  209.8 13.4 %copy-start.4 = (s32[4,2]{0,1:T(2,128)S(1)}, s32[4,2]{0,1:T(2,128)}, u32[]{:S(2)}) copy-start(s32[4,2]{0,1:T(2,128)} %param.15) | copy-start | bytes 100
  222.3 1.0 copy-start.1
Sparse Core Ops, SparseCore 0:
  223.4 54.5 reduce-scatter.1
where the time goes:
time: 294 us; the launch traced here: 290 us
  local copies, waits for them, and re-layouts  109 us (37%)
  waiting for transfers between devices  56.3 us (19%)
  matrix products  48.8 us (17%)
  blocking collectives  41.9 us (14%)
  starting transfers between devices  18 us (6%)
  between operations  13.6 us (5%)
    convert_element_type x2, local copies, waits for them, and re-layouts, operators(): return summed.astype(jnp.bfloat16)  66.3 us
    reduce_scatter x1, waiting for transfers between devices, local(): lax.psum_scatter(chi_cells, 'image', scatter_dimension=1, tiled=True)  54.4 us
    dot_general x1, matrix products, density_terms(): jnp.einsum('sjr,sjlm,sjnq->srlqmn', select, occ_vals.reshape(row_count, p...  33.8 us
    unnamed x13, local copies, waits for them, and re-layouts  26.4 us
    all_gather x1, blocking collectives, operators(): lax.all_gather(occ_local, 'image', axis=0, tiled=True)  25.9 us
    all_gather x1, blocking collectives, operators(): lax.all_gather(virt_local, 'image', axis=0, tiled=True)  15.9 us
    dot_general x4, matrix products, accumulate(): jnp.einsum('srkp,skq->rpq', mixed_rows, blk_part, preferred_element_type=...  12.3 us
    all_to_all x1, starting transfers between devices, local(): lax.all_to_all(packed_list.reshape(owners, capacity, listing.shape[1]), '...  10.5 us
  transfers between devices with their start and end apart: 3, of which 2 were waited for; matrix products, arithmetic and copies ran while one was open for 47% of the time, Pallas kernels for 0%

commit v1 on v0

v1 whole, which is shorter than its diff:
```python
import functools
import math

import jax
import jax.numpy as jnp
import numpy as np
from jax import lax
from jax.experimental import pallas as pl
from jax.experimental.pallas import tpu as pltpu
from jax.sharding import PartitionSpec as P

KGRID = 8
MESH = pl.DeviceIdType.MESH
NX, NY, NZ, NC = 4, 8, 8, 2
F32, BF16, I32 = jnp.float32, jnp.bfloat16, jnp.int32

ALT = [
    (0, 0), (1, 0), (-1, 0), (0, 1), (0, 3), (1, 1),
    (-1, 3), (1, 3), (-1, 1), (0, 2), (1, 2), (-1, 2),
]
HOME = [
    (0, 0), (2, 2), (-2, 2), (2, 3), (-2, 1), (2, 1), (-2, 3), (1, 2), (-1, 2), (2, 0),
    (-2, 0), (1, 1), (-1, 3), (1, 3), (-1, 1), (0, 2), (0, 1), (0, 3), (1, 0), (-1, 0),
]
NA, NH = len(ALT), len(HOME)
NPAIR = NA + NH


def position():
    i, r = lax.axis_index("image"), lax.axis_index("ri")
    return lax.div(i, NC), lax.rem(i, NC), lax.div(r, NX), lax.rem(r, NX)


def row_of(y, x, dy, dx):
    return lax.rem(y + dy + NY, NY) * NX + lax.rem(x + dx + NX, NX)


def main_kernel(
    lst_ref, occ_ref, virt_ref, blocks_ref, out_ref,
    packa, packh, recva, recvh, lsend, lrecv, pay, idxv, idxs,
    dens, sel, cel, ops, chia, chih,
    sa, sra, sh, srh, za, zra, zh, zrh, ex, exr, lists,
    idx_sem, as_sem, ar_sem, hs_sem, hr_sem, ls_sem, lr_sem,
    ds_sem, dr_sem, fs_sem, fr_sem,
    s_ssem, s_rsem, z_ssem, z_rsem, e_ssem, e_rsem,
):
    z, c, y, x = position()
    image, ri = lax.axis_index("image"), lax.axis_index("ri")
    sib = {"image": z * NC + (1 - c), "ri": ri}
    far = {"image": image, "ri": row_of(y, x, 4, 0)}

    def plane(off, sign=1):
        return {"image": image, "ri": row_of(y, x, sign * off[0], sign * off[1])}

    def zpeer(d):
        return {"image": lax.rem(z + d, NZ) * NC + c, "ri": ri}

    bar = pltpu.get_barrier_semaphore()
    peers = [plane(o) for o in HOME[1:]] + [zpeer(d) for d in range(1, NZ)] + [sib, far]
    for p in peers:
        pl.semaphore_signal(bar, inc=1, device_id=p, device_id_type=MESH)

    dens[image] = jnp.concatenate([occ_ref[0], virt_ref[0]], axis=1)
    lanes = lax.broadcasted_iota(I32, (32, 128), 1)
    erow = lax.broadcasted_iota(I32, (32, 128), 0)
    own = jnp.broadcast_to(lst_ref[:, 14:15], (32, 128)) == lanes
    lo = jnp.min(jnp.where(own, erow, 99), axis=0, keepdims=True)
    hi = jnp.max(jnp.where(own, erow, -1), axis=0, keepdims=True)
    idxv[0:1, :] = jnp.minimum(lo, 31)
    idxv[1:2, :] = jnp.maximum(hi, 0)
    to_smem = pltpu.make_async_copy(idxv, idxs, idx_sem)
    to_smem.start()
    fields = lst_ref[...].astype(F32).astype(BF16)
    for r, hit in ((0, erow == lo), (1, (erow == hi) & (hi != lo))):
        got = lax.dot_general(
            jnp.where(hit, 1.0, 0.0).astype(BF16), fields, (((0,), (0,)), ((), ())),
            preferred_element_type=F32,
        )
        pay[r] = got[0:32].astype(I32)
    for k, o in enumerate(HOME):
        o1, o2 = row_of(y, x, o[0], o[1]), row_of(y, x, o[0] + 4, o[1])
        dst = lrecv if k == 0 else lsend
        for s, (r, q) in enumerate(((0, o1), (1, o1), (0, o2), (1, o2))):
            dst[k, s : s + 1, :] = pay[r, pl.ds(q, 1), :]
    to_smem.wait()

    def pack(offs, shift, buf, local):
        for k, o in enumerate(offs):
            q = row_of(y, x, o[0] + shift, o[1])
            dst = local if k == 0 else buf
            for r in range(2):
                dst[k, r * 64 : (r + 1) * 64, :] = blocks_ref[idxs[r, q]]

    pack(ALT, 4, packa, recva)
    pl.semaphore_wait(bar, len(peers))

    def dcopy(d):
        return pltpu.make_async_remote_copy(
            dens.at[image], dens.at[image], ds_sem.at[d], dr_sem.at[d],
            device_id=zpeer(d), device_id_type=MESH,
        )

    def fcopy(d):
        src = dens.at[lax.rem(z + NZ - d, NZ) * NC + c]
        return pltpu.make_async_remote_copy(
            src, src, fs_sem.at[d], fr_sem.at[d], device_id=sib, device_id_type=MESH
        )

    def lcopy(k):
        return pltpu.make_async_remote_copy(
            lsend.at[k], lrecv.at[k], ls_sem.at[k], lr_sem.at[k],
            device_id=plane(HOME[k]), device_id_type=MESH,
        )

    def acopy(k):
        return pltpu.make_async_remote_copy(
            packa.at[k], recva.at[k], as_sem.at[k], ar_sem.at[k],
            device_id=plane(ALT[k]), device_id_type=MESH,
        )

    def hcopy(k):
        return pltpu.make_async_remote_copy(
            packh.at[k], recvh.at[k], hs_sem.at[k], hr_sem.at[k],
            device_id=plane(HOME[k]), device_id_type=MESH,
        )

    for d in (4, 3, 5, 2, 6, 1, 7):
        dcopy(d).start()
    fcopy(0).start()
    for k in range(1, NH):
        lcopy(k).start()
    for k in range(1, NA):
        acopy(k).start()
    pack(HOME, 0, packh, recvh)
    for k in range(1, NH):
        hcopy(k).start()

    rows2 = lax.broadcasted_iota(I32, (64, 256), 0)
    t = lax.rem(lax.broadcasted_iota(I32, (64, 256), 1), 128)
    xmask = ((t < 64) & (lax.rem(t, 8) == lax.div(rows2, 8))) | (
        (t >= 64) & (lax.div(t - 64, 8) == lax.rem(rows2, 8))
    )
    pi = lax.broadcasted_iota(I32, (256, 256), 0)
    pj = lax.broadcasted_iota(I32, (256, 256), 1)
    pt, u = lax.rem(pi, 128), lax.rem(pj, 64)
    same_r = lax.div(pi, 128) == lax.rem(lax.div(pj, 64), 2)
    occ_part = same_r & (pt < 64) & (pj < 128) & (lax.div(pt, 8) == lax.div(u, 8))
    virt_part = same_r & (pt >= 64) & (pj >= 128) & (lax.rem(pt, 8) == lax.rem(u, 8))
    spread = jnp.where(occ_part | virt_part, 1.0, 0.0).astype(BF16)
    eye = jnp.where(pi == pj, 1.0, 0.0).astype(BF16)

    for k in range(1, NH):
        lcopy(k).wait_recv()
    for n in range(NPAIR):
        k, s = (HOME.index(ALT[n]), 2) if n < NA else (n - NA, 0)
        for r in range(2):
            lists[r * 32 + n : r * 32 + n + 1, :] = lrecv[k, s + r : s + r + 1, :]
    fr = lists[...]
    low = lax.broadcasted_iota(I32, (32, 128), 1) < 64
    for j in range(4):
        cell = jnp.broadcast_to(fr[:, 10 + j : 11 + j], (64, 128))
        cel[j] = jnp.where(low, cell[0:32], cell[32:64])
    basis = lax.broadcasted_iota(I32, (64, 256), 1)
    pick = jnp.concatenate(
        [
            jnp.where(jnp.broadcast_to(fr[:, f : f + 1], (64, 256)) == basis, 1.0, 0.0)
            for f in range(2)
        ],
        axis=0,
    ).astype(BF16)

    for d in (1, 7, 2, 6, 3, 5, 4):
        dcopy(d).wait_recv()
        fcopy(d).start()
    for d in range(NZ):
        fcopy(d).wait_recv()
    sel[...] = jnp.zeros_like(sel)

    def choose(img, carry):
        d = jnp.dot(pick, dens[img], preferred_element_type=F32)
        for j in range(4):
            o_hit = jnp.broadcast_to(lists[:, 2 + j : 3 + j], (64, 128)) == img
            v_hit = jnp.broadcast_to(lists[:, 6 + j : 7 + j], (64, 128)) == img
            lane = lax.broadcasted_iota(I32, (64, 128), 1) < 64
            hit = (o_hit & lane) | (v_hit & jnp.logical_not(lane))
            val = jnp.where(lane, d[0:64], d[64:128])
            for r in range(2):
                rs = slice(r * 32, (r + 1) * 32)
                sel[j, :, r * 128 : (r + 1) * 128] = jnp.where(
                    hit[rs], val[rs], sel[j, :, r * 128 : (r + 1) * 128]
                )
        return carry

    lax.fori_loop(0, NZ * NC, choose, 0)

    def build(n, carry):
        acc = [jnp.zeros((64, 128), F32) for _ in range(4)]
        for j in range(4):
            row = jnp.broadcast_to(sel[j, pl.ds(n, 1), :], (64, 256))
            e = jnp.dot(jnp.where(xmask, row, 0.0).astype(BF16), spread, preferred_element_type=F32)
            kron = e[:, :128] * e[:, 128:]
            cell = jnp.broadcast_to(cel[j, pl.ds(n, 1), :], (64, 128))
            for q in range(4):
                acc[q] = acc[q] + jnp.where(cell == q + 1, kron, 0.0)
        lane = lax.broadcasted_iota(I32, (64, 128), 1) < 64
        for q in range(4):
            ls = slice(q * 128, (q + 1) * 128)
            ops[n, 0:64, ls] = jnp.where(lane, acc[q], 0.0).astype(BF16)
            ops[n, 64:128, ls] = jnp.where(lane, 0.0, acc[q]).astype(BF16)
        return carry

    lax.fori_loop(0, NPAIR, build, 0)

    def group(recv, chi, first, g):
        b = jnp.concatenate([recv[2 * g], recv[2 * g + 1]], axis=0)
        bt = lax.dot_general(eye, b, (((1,), (1,)), ((), ())), preferred_element_type=F32)
        bt = bt.astype(BF16)
        mixed = [
            jnp.dot(
                bt[:, i * 128 : (i + 1) * 128], ops[first + 2 * g + i], preferred_element_type=F32
            ).astype(BF16)
            for i in range(2)
        ]
        for q in range(4):
            ls = slice(q * 128, (q + 1) * 128)
            m = jnp.concatenate([mixed[0][:, ls], mixed[1][:, ls]], axis=1)
            chi[q] += jnp.dot(m, b, preferred_element_type=F32)

    def wait_pair(recv, sem, n):
        pltpu.make_async_remote_copy(
            recv.at[n], recv.at[n], sem.at[n], sem.at[n], device_id=sib, device_id_type=MESH
        ).wait_recv()

    def run_groups(recv, sem, chi, first, start, stop):
        def body(g, carry):
            @pl.when(g > 0)
            def _():
                wait_pair(recv, sem, 2 * g)

            wait_pair(recv, sem, 2 * g + 1)
            group(recv, chi, first, g)
            return carry

        lax.fori_loop(start, stop, body, 0)

    def scopy(buf, rbuf, w):
        return pltpu.make_async_remote_copy(
            buf, rbuf, s_ssem.at[w], s_rsem.at[w], device_id=sib, device_id_type=MESH
        )

    def zcopy(buf, rbuf, w, d):
        return pltpu.make_async_remote_copy(
            buf.at[d], rbuf.at[d], z_ssem.at[w, d], z_rsem.at[w, d],
            device_id=zpeer(d), device_id_type=MESH,
        )

    def share_rows(d, core):
        zz = lax.rem(z + d, NZ)
        return pl.ds(pl.multiple_of((zz * NC + core) * 16, 16), 16)

    def to_sibling(chi, buf, rbuf, w):
        def body(d, carry):
            buf[d] = chi[:, share_rows(d, 1 - c), :].astype(BF16)
            return carry

        lax.fori_loop(0, NZ, body, 0)
        scopy(buf, rbuf, w).start()

    def to_chips(chi, buf, rbuf, zbuf, w):
        scopy(buf, rbuf, w).wait_recv()

        def body(d, carry):
            zbuf[d] = (chi[:, share_rows(d, c), :] + rbuf[d].astype(F32)).astype(BF16)
            return carry

        lax.fori_loop(1, NZ, body, 0)
        return chi[:, share_rows(0, c), :] + rbuf[0].astype(F32)

    chia[...] = jnp.zeros_like(chia)
    chih[...] = jnp.zeros_like(chih)
    run_groups(recva, ar_sem, chia, 0, 0, NA // 2)
    to_sibling(chia, sa, sra, 0)
    run_groups(recvh, hr_sem, chih, NA, 0, 3)
    out_ref[...] = to_chips(chia, sa, sra, za, 0)
    for d in (4, 3, 5, 2, 6, 1, 7):
        zcopy(za, zra, 0, d).start()
    run_groups(recvh, hr_sem, chih, NA, 3, 7)
    total = out_ref[...]
    for d in range(1, NZ):
        zcopy(za, zra, 0, d).wait_recv()
        total = total + zra[d].astype(F32)
    ex[...] = total.astype(BF16)
    to_far = pltpu.make_async_remote_copy(
        ex, exr, e_ssem, e_rsem, device_id=far, device_id_type=MESH
    )
    to_far.start()
    run_groups(recvh, hr_sem, chih, NA, 7, NH // 2)
    to_sibling(chih, sh, srh, 1)
    mine = to_chips(chih, sh, srh, zh, 1)
    for d in (4, 3, 5, 2, 6, 1, 7):
        zcopy(zh, zrh, 1, d).start()
    to_far.wait_recv()
    mine = mine + exr[...].astype(F32)
    for d in (1, 7, 2, 6, 3, 5, 4):
        zcopy(zh, zrh, 1, d).wait_recv()
        mine = mine + zrh[d].astype(F32)
    out_ref[...] = mine

    for d in range(1, NZ):
        dcopy(d).wait_send()
        zcopy(za, zra, 0, d).wait_send()
        zcopy(zh, zrh, 1, d).wait_send()
    for d in range(NZ):
        fcopy(d).wait_send()
    for k in range(1, NH):
        lcopy(k).wait_send()
        hcopy(k).wait_send()
    for k in range(1, NA):
        acopy(k).wait_send()
    scopy(sa, sra, 0).wait_send()
    scopy(sh, srh, 1).wait_send()
    to_far.wait_send()


def phase_kernel(lat_ref, cos_ref, chi_ref, out_ref):
    part = pl.program_id(0)
    n = out_ref.shape[1]

    def body(i, carry):
        k = part * n + i
        k1, k2 = lax.div(k, KGRID), lax.rem(k, KGRID)
        re = jnp.zeros(chi_ref.shape[1:], F32)
        im = jnp.zeros(chi_ref.shape[1:], F32)
        for r in range(chi_ref.shape[0]):
            w = lax.rem(k1 * lat_ref[r, 0] + k2 * lat_ref[r, 1] + 64 * KGRID, KGRID)
            piece = chi_ref[r]
            re = re + cos_ref[w] * piece
            im = im + cos_ref[lax.rem(w + 6, KGRID)] * piece
        out_ref[0, i, 0] = re
        out_ref[1, i, 0] = im
        return carry

    lax.fori_loop(0, n, body, 0, unroll=True)


def local(blocks, block_owner, block_basis, pair_images, pair_cell, lattice, dens_occ, dens_virt):
    rows, square, width = blocks.shape
    cells = lattice.shape[0]
    listing = jnp.concatenate(
        [block_basis, pair_images.reshape(rows, -1), pair_cell + 1, block_owner], axis=1
    )
    listing = jnp.pad(listing, ((0, 0), (0, 128 - listing.shape[1])))
    vm = pltpu.VMEM
    dma = pltpu.SemaphoreType.DMA
    share = (NZ, cells, 16, width)
    chi = pl.pallas_call(
        main_kernel,
        out_shape=jax.ShapeDtypeStruct((cells, 16, width), F32),
        in_specs=[pl.BlockSpec(memory_space=pltpu.VMEM)] * 4,
        out_specs=pl.BlockSpec(memory_space=pltpu.VMEM),
        scratch_shapes=[
            vm((NA, 128, width), BF16),
            vm((NH, 128, width), BF16),
            vm((NA, 128, width), BF16),
            vm((NH, 128, width), BF16),
            vm((NH, 8, 128), I32),
            vm((NH, 8, 128), I32),
            vm((2, 32, 128), I32),
            vm((8, 128), I32),
            pltpu.SMEM((8, 128), I32),
            vm((NZ * NC, 256, 128), BF16),
            vm((4, NPAIR, 256), F32),
            vm((4, NPAIR, 128), I32),
            vm((NPAIR, 128, 512), BF16),
            vm((cells, width, width), F32),
            vm((cells, width, width), F32),
        ]
        + [vm(share, BF16)] * 8
        + [vm(share[1:], BF16)] * 2
        + [vm((64, 128), I32)]
        + [
            dma(()),
            dma((NA,)), dma((NA,)), dma((NH,)), dma((NH,)), dma((NH,)), dma((NH,)),
            dma((NZ,)), dma((NZ,)), dma((NZ,)), dma((NZ,)),
            dma((2,)), dma((2,)), dma((2, NZ)), dma((2, NZ)), dma(()), dma(()),
        ],
        compiler_params=pltpu.CompilerParams(
            collective_id=0, has_side_effects=True, vmem_limit_bytes=48 << 20
        ),
    )(listing, dens_occ, dens_virt, blocks)
    table = jnp.asarray(np.cos(2.0 * math.pi / KGRID * np.arange(KGRID)), F32)
    points = KGRID * KGRID
    parts = 8
    return pl.pallas_call(
        phase_kernel,
        out_shape=jax.ShapeDtypeStruct((2, points, 1, 16, width), F32),
        grid=(parts,),
        in_specs=[
            pl.BlockSpec(memory_space=pltpu.SMEM),
            pl.BlockSpec(memory_space=pltpu.SMEM),
            pl.BlockSpec((cells, 16, width), lambda i: (0, 0, 0)),
        ],
        out_specs=pl.BlockSpec((2, points // parts, 1, 16, width), lambda i: (0, i, 0, 0, 0)),
    )(lattice, table, chi)


def solution(mesh):
    both = ("image", "ri")
    placed = (
        P(both, None, None),
        P(both, None),
        P(both, None),
        P(both, None, None),
        P(both, None),
        P(),
        P("image", None, None),
        P("image", None, None),
    )
    return jax.shard_map(
        local,
        mesh=mesh,
        in_specs=placed,
        out_specs=P(None, None, "ri", "image", None),
        check_vma=False,
    )
```

time: 294 us -> 81.5 us (0.28); the launches traced: 290 us -> 81 us
  local copies, waits for them, and re-layouts: 109 us -> 7.28 us
  Pallas kernels: 0 us -> 72.9 us
  waiting for transfers between devices: 56.3 us -> 0 us
  matrix products: 48.8 us -> 0 us
  blocking collectives: 41.9 us -> 0 us
  starting transfers between devices: 18 us -> 0 us
  between operations: 13.6 us -> 0.04 us
    pallas_call x0 -> x2, Pallas kernels: none -> 72.9 us  [the longest x1 68.2 us: local(): pl.pallas_call(main_kernel, out_shape=jax.ShapeDtypeStruct((cells, 16, wi...]
    convert_element_type x4 -> x0, local copies, waits for them, and re-layouts: 66.7 us -> none  [the longest x2 66.3 us: operators(): return summed.astype(jnp.bfloat16)]
    reduce_scatter x1 -> x0, waiting for transfers between devices: 54.4 us -> none  [local(): lax.psum_scatter(chi_cells, 'image', scatter_dimension=1, tiled=True)]
    dot_general x6 -> x0, matrix products: 48.8 us -> none  [the longest x1 33.8 us: density_terms(): jnp.einsum('sjr,sjlm,sjnq->srlqmn', select, occ_vals.reshape(row_count, p...]
    all_gather x2 -> x0, blocking collectives: 41.9 us -> none  [the longest x1 25.9 us: operators(): lax.all_gather(occ_local, 'image', axis=0, tiled=True)]
    unnamed x13 -> x9, local copies, waits for them, and re-layouts: 26.4 us -> 6.42 us
    all_to_all x2 -> x0, starting transfers between devices: 18 us -> none  [the longest x1 10.5 us: local(): lax.all_to_all(packed_list.reshape(owners, capacity, listing.shape[1]), '...]
    scatter x2 -> x0, local copies, waits for them, and re-layouts: 6.46 us -> none  [the longest x1 5.24 us: local(): jnp.zeros((slot_count, square, ri_width), blocks.dtype).at[slot_index]]
  transfers between devices with their start and end apart: 3 -> 0, of which waited for: 2 -> 0; matrix products, arithmetic and copies ran while one was open for 47% -> 0% of each run, Pallas kernels for 0% -> 0%
where the time goes in v1:
time: 81.5 us; the launch traced here: 81 us
  Pallas kernels  72.9 us (89%)
  local copies, waits for them, and re-layouts  7.28 us (9%)
    pallas_call x1, Pallas kernels, local(): pl.pallas_call(main_kernel, out_shape=jax.ShapeDtypeStruct((cells, 16, wi...  68.2 us
    unnamed x9, local copies, waits for them, and re-layouts  6.42 us
    pallas_call x1, Pallas kernels, local(): pl.pallas_call(phase_kernel, out_shape=jax.ShapeDtypeStruct((2, points, 1...  4.76 us

profile of v1, /device:TPU:1, one launch (start us, length us, event | category | flops | bytes accessed | tf_op | source)
XLA Modules:
  0.0 81.0 jit_solution(9397317953515497117)
XLA Ops:
  0.0 0.7 broadcast_add_fusion
  0.7 1.4 %copy.32.lat_ref = s32[4,2]{1,0:T(4,128)} copy(s32[4,2]{0,1:T(2,128)} %param.14) | data formatting | bytes 64 | tf_op args[5]
  2.0 0.1 copy.28
  2.1 0.7 copy.29
  2.9 0.8 copy.26
  3.6 0.8 copy.27
  4.4 0.1 pad_add_fusion
  4.5 0.9 %copy.30.occ_ref = bf16[1,256,64]{2,1,0:T(8,128)(2,1)S(1)} copy(bf16[1,256,64]{1,2,0:T(8,128)(2,1)} %param.15) | data formatting | bytes 65536 | tf_op args[6]
  5.3 0.9 %copy.31.virt_ref = bf16[1,256,64]{2,1,0:T(8,128)(2,1)S(1)} copy(bf16[1,256,64]{1,2,0:T(8,128)(2,1)} %param.16) | data formatting | bytes 65536 | tf_op args[7]
  6.2 0.0 copy-start
  6.2 1.2 %copy-done = bf16[32,64,256]{2,1,0:T(8,128)(2,1)S(1)} copy-done((bf16[32,64,256]{2,1,0:T(8,128)(2,1)S(1)}, bf16[32,64,256]{2,1,0:T(8,128)(2,1)}, u32[]{:S(2)}) %copy-start) | copy-done | bytes 1048600
  7.5 68.2 %shard_map.91.chi_ref = f32[4,16,256]{2,1,0:T(8,128)S(1)} custom-call(s32[32,128]{1,0:T(8,128)S(1)} %pad.4.lst_ref, bf16[1,256,64]{2,1,0:T(8,128)(2,1)S(1)} %copy.30.occ_ref, bf16[1,256,64]{2,1,0:T(8,128)(2,1)S(1)} %copy.31.virt_ref, bf16[32,64,256]{2,1,0:T(8,128)(2,1)S(1)} %copy-done), custom_call_target="tpu_custom_call" | custom-call | tf_op jit(solution)/shard_map/pallas_call | solution.py:356
  75.7 0.0 copy-start.1
  75.7 0.6 copy-done.1
  76.3 4.8 %shard_map.92 = f32[2,64,1,16,256]{4,3,2,1,0:T(8,128)} custom-call(s32[4,2]{1,0:T(4,128)} %copy.32.lat_ref, f32[8]{0:T(128)} %constant.6.clone.cos_ref, f32[4,16,256]{2,1,0:T(8,128)} %copy-done.1), custom_call_target="tpu_custom_call" | custom-call | tf_op jit(solution)/shard_map/pallas_call | solution.py:394
  (1 shorter events, 0.0 us)
Async XLA Ops:
  6.2 1.2 %copy-start = (bf16[32,64,256]{2,1,0:T(8,128)(2,1)S(1)}, bf16[32,64,256]{2,1,0:T(8,128)(2,1)}, u32[]{:S(2)}) copy-start(bf16[32,64,256]{2,1,0:T(8,128)(2,1)} %blocks_ref.1) | copy-start | bytes 3145732
  75.7 0.6 copy-start.1

commit v2 on v1

v2 whole, which is shorter than its diff:
```python
import functools
import math

import jax
import jax.numpy as jnp
import numpy as np
from jax import lax
from jax.experimental import pallas as pl
from jax.experimental.pallas import tpu as pltpu
from jax.sharding import PartitionSpec as P

KGRID = 8
MESH = pl.DeviceIdType.MESH
NX, NY, NZ, NC = 4, 8, 8, 2
F32, BF16, I32 = jnp.float32, jnp.bfloat16, jnp.int32

ALT = [
    (0, 0), (1, 0), (-1, 0), (0, 1), (0, 3), (1, 1),
    (-1, 3), (1, 3), (-1, 1), (0, 2), (1, 2), (-1, 2),
]
HOME = [
    (0, 0), (2, 2), (-2, 2), (2, 3), (-2, 1), (2, 1), (-2, 3), (1, 2), (-1, 2), (2, 0),
    (-2, 0), (1, 1), (-1, 3), (1, 3), (-1, 1), (0, 2), (0, 1), (0, 3), (1, 0), (-1, 0),
]
NA, NH = len(ALT), len(HOME)
NPAIR = NA + NH


def position():
    i, r = lax.axis_index("image"), lax.axis_index("ri")
    return lax.div(i, NC), lax.rem(i, NC), lax.div(r, NX), lax.rem(r, NX)


def row_of(y, x, dy, dx):
    return lax.rem(y + dy + NY, NY) * NX + lax.rem(x + dx + NX, NX)


def main_kernel(
    owner_hbm, basis_hbm, images_hbm, cell_hbm, occ_hbm, virt_hbm, blocks_hbm, out_hbm,
    owner_ref, basis_ref, images_ref, cell_ref, blk, out_ref,    packa, packh, recva, recvh, lsend, lrecv, pay, idxv, idxs,
    dens, sel, want, cel, ops, chia, chih,
    sa, sra, sh, srh, za, zra, zh, zrh, ex, exr, lists,
    in_sem, idx_sem, as_sem, ar_sem, hs_sem, hr_sem, ls_sem, lr_sem,
    ds_sem, dr_sem, fs_sem, fr_sem,
    s_ssem, s_rsem, z_ssem, z_rsem, e_ssem, e_rsem,
):
    z, c, y, x = position()
    image, ri = lax.axis_index("image"), lax.axis_index("ri")
    sib = {"image": z * NC + (1 - c), "ri": ri}
    far = {"image": image, "ri": row_of(y, x, 4, 0)}

    def plane(off, sign=1):
        return {"image": image, "ri": row_of(y, x, sign * off[0], sign * off[1])}

    def zpeer(d):
        return {"image": lax.rem(z + d, NZ) * NC + c, "ri": ri}

    loads = [
        pltpu.make_async_copy(src, dst, in_sem.at[i])
        for i, (src, dst) in enumerate(
            (
                (owner_hbm, owner_ref),
                (basis_hbm, basis_ref),
                (images_hbm, images_ref),
                (cell_hbm, cell_ref),
                (occ_hbm.at[0], dens.at[image, 0:64]),
                (virt_hbm.at[0], dens.at[image, 64:128]),
                (blocks_hbm, blk),
            )
        )
    ]
    for cp in loads:
        cp.start()

    bar = pltpu.get_barrier_semaphore()
    peers = [plane(o) for o in HOME[1:]] + [zpeer(d) for d in range(1, NZ)] + [sib, far]
    for p in peers:
        pl.semaphore_signal(bar, inc=1, device_id=p, device_id_type=MESH)

    for cp in loads[:4]:
        cp.wait()
    orow = lax.broadcasted_iota(I32, (32, 32), 0)
    ecol = lax.broadcasted_iota(I32, (32, 32), 1)
    own = jnp.broadcast_to(owner_ref[...], (32, 32)) == orow
    lo = jnp.min(jnp.where(own, ecol, 99), axis=1, keepdims=True)
    hi = jnp.max(jnp.where(own, ecol, -1), axis=1, keepdims=True)
    lane = lax.broadcasted_iota(I32, (32, 128), 1)
    idxv[...] = jnp.where(lane == 0, jnp.minimum(lo, 31), jnp.maximum(hi, 0))
    to_smem = pltpu.make_async_copy(idxv, idxs, idx_sem)
    to_smem.start()
    fields = jnp.concatenate(
        [basis_ref[...], images_ref[0], images_ref[1], cell_ref[...] + 1], axis=0
    ).astype(F32)
    for r, hit in ((0, ecol == lo), (1, (ecol == hi) & (hi != lo))):
        got = lax.dot_general(
            jnp.where(hit, 1.0, 0.0), fields, (((1,), (1,)), ((), ())),
            preferred_element_type=F32,
        )
        pay[r, :, 0:14] = got.astype(I32)
    def dcopy(d):
        return pltpu.make_async_remote_copy(
            dens.at[image], dens.at[image], ds_sem.at[d], dr_sem.at[d],
            device_id=zpeer(d), device_id_type=MESH,
        )

    def fcopy(d):
        src = dens.at[lax.rem(z + NZ - d, NZ) * NC + c]
        return pltpu.make_async_remote_copy(
            src, src, fs_sem.at[d], fr_sem.at[d], device_id=sib, device_id_type=MESH
        )

    def lcopy(k):
        return pltpu.make_async_remote_copy(
            lsend.at[k], lrecv.at[k], ls_sem.at[k], lr_sem.at[k],
            device_id=plane(HOME[k]), device_id_type=MESH,
        )

    def acopy(k):
        return pltpu.make_async_remote_copy(
            packa.at[k], recva.at[k], as_sem.at[k], ar_sem.at[k],
            device_id=plane(ALT[k]), device_id_type=MESH,
        )

    def hcopy(k):
        return pltpu.make_async_remote_copy(
            packh.at[k], recvh.at[k], hs_sem.at[k], hr_sem.at[k],
            device_id=plane(HOME[k]), device_id_type=MESH,
        )

    def pack(k, off, shift, buf, local):
        q = row_of(y, x, off[0] + shift, off[1])
        dst = local if k == 0 else buf
        for r in range(2):
            dst[k, r * 64 : (r + 1) * 64, :] = blk[idxs[q, r]]

    for k, o in enumerate(HOME):
        o1, o2 = row_of(y, x, o[0], o[1]), row_of(y, x, o[0] + 4, o[1])
        dst = lrecv if k == 0 else lsend
        for s, (r, q) in enumerate(((0, o1), (1, o1), (0, o2), (1, o2))):
            dst[k, s : s + 1, :] = pay[r, pl.ds(q, 1), :]
    to_smem.wait()
    for cp in loads[4:]:
        cp.wait()
    for k in range(NA):
        pack(k, ALT[k], 4, packa, recva)
    pl.semaphore_wait(bar, len(peers))
    for d in (4, 3, 5, 2, 6, 1, 7):
        dcopy(d).start()
    fcopy(0).start()
    for k in range(1, NH):
        lcopy(k).start()
    for k in range(1, NA):
        acopy(k).start()
    for k in range(NH):
        pack(k, HOME[k], 0, packh, recvh)
    for k in range(1, NH):
        hcopy(k).start()

    rows2 = lax.broadcasted_iota(I32, (64, 256), 0)
    t = lax.rem(lax.broadcasted_iota(I32, (64, 256), 1), 128)
    xmask = ((t < 64) & (lax.rem(t, 8) == lax.div(rows2, 8))) | (
        (t >= 64) & (lax.div(t - 64, 8) == lax.rem(rows2, 8))
    )
    pi = lax.broadcasted_iota(I32, (256, 256), 0)
    pj = lax.broadcasted_iota(I32, (256, 256), 1)
    pt, u = lax.rem(pi, 128), lax.rem(pj, 64)
    same_r = lax.div(pi, 128) == lax.rem(lax.div(pj, 64), 2)
    occ_part = same_r & (pt < 64) & (pj < 128) & (lax.div(pt, 8) == lax.div(u, 8))
    virt_part = same_r & (pt >= 64) & (pj >= 128) & (lax.rem(pt, 8) == lax.rem(u, 8))
    spread = jnp.where(occ_part | virt_part, 1.0, 0.0).astype(BF16)

    for k in range(1, NH):
        lcopy(k).wait_recv()
    for n in range(NPAIR):
        k, s = (HOME.index(ALT[n]), 2) if n < NA else (n - NA, 0)
        for r in range(2):
            lists[r * 32 + n : r * 32 + n + 1, :] = lrecv[k, s + r : s + r + 1, :]
    fr = lists[...]
    low = lax.broadcasted_iota(I32, (32, 128), 1) < 64
    for j in range(4):
        cell = jnp.broadcast_to(fr[:, 10 + j : 11 + j], (64, 128))
        cel[j] = jnp.where(low, cell[0:32], cell[32:64])
    basis = lax.broadcasted_iota(I32, (64, 256), 1)
    pick = jnp.concatenate(
        [
            jnp.where(jnp.broadcast_to(fr[:, f : f + 1], (64, 256)) == basis, 1.0, 0.0)
            for f in range(2)
        ],
        axis=0,
    ).astype(BF16)

    lane64 = lax.broadcasted_iota(I32, (64, 128), 1) < 64
    for j in range(4):
        want[j] = jnp.where(
            lane64,
            jnp.broadcast_to(fr[:, 2 + j : 3 + j], (64, 128)),
            jnp.broadcast_to(fr[:, 6 + j : 7 + j], (64, 128)),
        )
    sel[...] = jnp.zeros_like(sel)

    def choose(d, core):
        img = lax.rem(z + NZ - d, NZ) * NC + core
        v = lax.dot_general(
            pick, dens[img], (((1,), (1,)), ((), ())), preferred_element_type=F32
        )
        v = jnp.where(lane64, v[0:64], v[64:128])
        for j in range(4):
            hit = want[j] == img
            for r in range(2):
                rs, ls = slice(r * 32, (r + 1) * 32), slice(r * 128, (r + 1) * 128)
                sel[j, :, ls] = jnp.where(hit[rs], v[rs], sel[j, :, ls])

    choose(0, c)
    last = 0
    for d in (1, 7, 2, 6, 3, 5, 4):
        dcopy(d).wait_recv()
        fcopy(d).start()
        choose(d, c)
        fcopy(last).wait_recv()
        choose(last, 1 - c)
        last = d
    fcopy(last).wait_recv()
    choose(last, 1 - c)

    def build(n, carry):
        spot = jnp.concatenate(
            [
                jnp.where(xmask, jnp.broadcast_to(sel[j, pl.ds(n, 1), :], (64, 256)), 0.0)
                for j in range(4)
            ],
            axis=0,
        ).astype(BF16)
        e = jnp.dot(spot, spread, preferred_element_type=F32)
        kron = e[:, :128] * e[:, 128:]
        acc = [jnp.zeros((64, 128), F32) for _ in range(4)]
        for j in range(4):
            cell = jnp.broadcast_to(cel[j, pl.ds(n, 1), :], (64, 128))
            for q in range(4):
                acc[q] = acc[q] + jnp.where(cell == q + 1, kron[j * 64 : (j + 1) * 64], 0.0)
        for q in range(4):
            ls = slice(q * 128, (q + 1) * 128)
            ops[n, 0:64, ls] = jnp.where(lane64, acc[q], 0.0).astype(BF16)
            ops[n, 64:128, ls] = jnp.where(lane64, 0.0, acc[q]).astype(BF16)
        return carry

    lax.fori_loop(0, NPAIR, build, 0, unroll=4)

    def group(recv, chi, first, g):
        b = jnp.concatenate([recv[4 * g + i] for i in range(4)], axis=0)
        bt = b.T
        mixed = [
            jnp.dot(
                bt[:, i * 128 : (i + 1) * 128], ops[first + 4 * g + i], preferred_element_type=F32
            ).astype(BF16)
            for i in range(4)
        ]
        for q in range(4):
            m = jnp.concatenate([p[:, q * 128 : (q + 1) * 128] for p in mixed], axis=1)
            chi[q] += jnp.dot(m, b, preferred_element_type=F32)

    def wait_pair(recv, sem, n):
        pltpu.make_async_remote_copy(
            recv.at[n], recv.at[n], sem.at[n], sem.at[n], device_id=sib, device_id_type=MESH
        ).wait_recv()

    def run_groups(recv, sem, chi, first, start, stop):
        def body(g, carry):
            @pl.when(g > 0)
            def _():
                wait_pair(recv, sem, 4 * g)

            for i in range(1, 4):
                wait_pair(recv, sem, 4 * g + i)
            group(recv, chi, first, g)
            return carry

        lax.fori_loop(start, stop, body, 0)

    def scopy(buf, rbuf, w):
        return pltpu.make_async_remote_copy(
            buf, rbuf, s_ssem.at[w], s_rsem.at[w], device_id=sib, device_id_type=MESH
        )

    def zcopy(buf, rbuf, w, d):
        return pltpu.make_async_remote_copy(
            buf.at[d], rbuf.at[d], z_ssem.at[w, d], z_rsem.at[w, d],
            device_id=zpeer(d), device_id_type=MESH,
        )

    def share_rows(d, core):
        zz = lax.rem(z + d, NZ)
        return pl.ds(pl.multiple_of((zz * NC + core) * 16, 16), 16)

    def to_sibling(chi, buf, rbuf, w):
        def body(d, carry):
            buf[d] = chi[:, share_rows(d, 1 - c), :].astype(BF16)
            return carry

        lax.fori_loop(0, NZ, body, 0)
        scopy(buf, rbuf, w).start()

    def to_chips(chi, buf, rbuf, zbuf, w):
        scopy(buf, rbuf, w).wait_recv()

        def body(d, carry):
            zbuf[d] = (chi[:, share_rows(d, c), :] + rbuf[d].astype(F32)).astype(BF16)
            return carry

        lax.fori_loop(1, NZ, body, 0)
        return chi[:, share_rows(0, c), :] + rbuf[0].astype(F32)

    chia[...] = jnp.zeros_like(chia)
    chih[...] = jnp.zeros_like(chih)
    run_groups(recva, ar_sem, chia, 0, 0, NA // 4)
    to_sibling(chia, sa, sra, 0)
    run_groups(recvh, hr_sem, chih, NA, 0, 1)
    out_ref[...] = to_chips(chia, sa, sra, za, 0)
    for d in (4, 3, 5, 2, 6, 1, 7):
        zcopy(za, zra, 0, d).start()
    run_groups(recvh, hr_sem, chih, NA, 1, 3)
    total = out_ref[...]
    for d in range(1, NZ):
        zcopy(za, zra, 0, d).wait_recv()
        total = total + zra[d].astype(F32)
    ex[...] = total.astype(BF16)
    to_far = pltpu.make_async_remote_copy(
        ex, exr, e_ssem, e_rsem, device_id=far, device_id_type=MESH
    )
    to_far.start()
    run_groups(recvh, hr_sem, chih, NA, 3, NH // 4)
    to_sibling(chih, sh, srh, 1)
    mine = to_chips(chih, sh, srh, zh, 1)
    for d in (4, 3, 5, 2, 6, 1, 7):
        zcopy(zh, zrh, 1, d).start()
    to_far.wait_recv()
    mine = mine + exr[...].astype(F32)
    for d in (1, 7, 2, 6, 3, 5, 4):
        zcopy(zh, zrh, 1, d).wait_recv()
        mine = mine + zrh[d].astype(F32)
    out_ref[...] = mine
    result = pltpu.make_async_copy(out_ref, out_hbm, in_sem.at[7])
    result.start()

    for d in range(1, NZ):
        dcopy(d).wait_send()
        zcopy(za, zra, 0, d).wait_send()
        zcopy(zh, zrh, 1, d).wait_send()
    for d in range(NZ):
        fcopy(d).wait_send()
    for k in range(1, NH):
        lcopy(k).wait_send()
        hcopy(k).wait_send()
    for k in range(1, NA):
        acopy(k).wait_send()
    scopy(sa, sra, 0).wait_send()
    scopy(sh, srh, 1).wait_send()
    to_far.wait_send()
    result.wait()


def phase_kernel(lat_ref, cos_ref, chi_ref, out_ref, buf, sem):
    points, parts = KGRID * KGRID, sem.shape[0]
    n = points // parts
    cells = chi_ref.shape[0]
    pieces = [chi_ref[r] for r in range(cells)]
    lat = [(lat_ref[0, r], lat_ref[1, r]) for r in range(cells)]

    def copy(i):
        ks = slice(i * n, (i + 1) * n)
        return pltpu.make_async_copy(buf.at[:, ks], out_ref.at[:, ks], sem.at[i])

    for k in range(points):
        k1, k2 = k // KGRID, k % KGRID
        re = im = None
        for r in range(cells):
            w = (k1 * lat[r][0] + k2 * lat[r][1]) & (KGRID - 1)
            a, b = cos_ref[w] * pieces[r], cos_ref[(w + 6) & (KGRID - 1)] * pieces[r]
            re, im = (a, b) if re is None else (re + a, im + b)
        buf[0, k, 0] = re
        buf[1, k, 0] = im
        if k % n == n - 1:
            copy(k // n).start()
    for i in range(parts):
        copy(i).wait()


def local(blocks, block_owner, block_basis, pair_images, pair_cell, lattice, dens_occ, dens_virt):
    width = blocks.shape[2]
    cells = lattice.shape[0]
    vm = pltpu.VMEM
    dma = pltpu.SemaphoreType.DMA
    share = (NZ, cells, 16, width)
    chi = pl.pallas_call(
        main_kernel,
        out_shape=jax.ShapeDtypeStruct((cells, 16, width), F32),
        in_specs=[pl.BlockSpec(memory_space=pltpu.HBM)] * 7,
        out_specs=pl.BlockSpec(memory_space=pltpu.HBM),
        scratch_shapes=[
            vm((1, 32), I32),
            vm((2, 32), I32),
            vm((2, 4, 32), I32),
            vm((4, 32), I32),
            vm((32, 64, width), BF16),
            vm((cells, 16, width), F32),
            vm((NA, 128, width), BF16),
            vm((NH, 128, width), BF16),
            vm((NA, 128, width), BF16),
            vm((NH, 128, width), BF16),
            vm((NH, 8, 128), I32),
            vm((NH, 8, 128), I32),
            vm((2, 32, 128), I32),
            vm((32, 128), I32),
            pltpu.SMEM((32, 128), I32),
            vm((NZ * NC, 128, 256), BF16),
            vm((4, NPAIR, 256), F32),
            vm((4, 2 * NPAIR, 128), I32),
            vm((4, NPAIR, 128), I32),
            vm((NPAIR, 128, 512), BF16),
            vm((cells, width, width), F32),
            vm((cells, width, width), F32),
        ]
        + [vm(share, BF16)] * 8
        + [vm(share[1:], BF16)] * 2
        + [vm((64, 128), I32)]
        + [
            dma((8,)), dma(()),
            dma((NA,)), dma((NA,)), dma((NH,)), dma((NH,)), dma((NH,)), dma((NH,)),
            dma((NZ,)), dma((NZ,)), dma((NZ,)), dma((NZ,)),
            dma((2,)), dma((2,)), dma((2, NZ)), dma((2, NZ)), dma(()), dma(()),
        ],
        compiler_params=pltpu.CompilerParams(
            collective_id=0, has_side_effects=True, vmem_limit_bytes=60 << 20
        ),
    )(
        block_owner.T, block_basis.T, jnp.transpose(pair_images, (1, 2, 0)), pair_cell.T,
        jnp.swapaxes(dens_occ, 1, 2), jnp.swapaxes(dens_virt, 1, 2), blocks,
    )
    table = jnp.asarray(np.cos(2.0 * math.pi / KGRID * np.arange(KGRID)), F32)
    full = (2, KGRID * KGRID, 1, 16, width)
    return pl.pallas_call(
        phase_kernel,
        out_shape=jax.ShapeDtypeStruct(full, F32),
        in_specs=[
            pl.BlockSpec(memory_space=pltpu.SMEM),
            pl.BlockSpec(memory_space=pltpu.SMEM),
            pl.BlockSpec(memory_space=pltpu.VMEM),
        ],
        out_specs=pl.BlockSpec(memory_space=pl.ANY),
        scratch_shapes=[pltpu.VMEM(full, F32), pltpu.SemaphoreType.DMA((8,))],
    )(lattice.T, table, chi)


def solution(mesh):
    both = ("image", "ri")
    placed = (
        P(both, None, None),
        P(both, None),
        P(both, None),
        P(both, None, None),
        P(both, None),
        P(),
        P("image", None, None),
        P("image", None, None),
    )
    return jax.shard_map(
        local,
        mesh=mesh,
        in_specs=placed,
        out_specs=P(None, None, "ri", "image", None),
        check_vma=False,
    )
```

time: 81.5 us -> 65.2 us (0.80)
  Pallas kernels: 72.9 us -> 65.1 us
  local copies, waits for them, and re-layouts: 7.28 us -> 0 us
    unnamed x9 -> x0, local copies, waits for them, and re-layouts: 6.42 us -> none
    pallas_call x1, Pallas kernels: 68.2 us -> 62.8 us  [local(): pl.pallas_call(main_kernel, out_shape=jax.ShapeDtypeStruct((cells, 16, wi...]
    pallas_call x1, Pallas kernels: 4.76 us -> 2.3 us  [local(): pl.pallas_call(phase_kernel, out_shape=jax.ShapeDtypeStruct(full, F32), i...]
where the time goes in v2:
time: 65.2 us; the launch traced here: 65.1 us
  Pallas kernels  65.1 us (100%)
    pallas_call x1, Pallas kernels, local(): pl.pallas_call(main_kernel, out_shape=jax.ShapeDtypeStruct((cells, 16, wi...  62.8 us
    pallas_call x1, Pallas kernels, local(): pl.pallas_call(phase_kernel, out_shape=jax.ShapeDtypeStruct(full, F32), i...  2.3 us

profile of v2, /device:TPU:1, one launch (start us, length us, event | category | flops | bytes accessed | tf_op | source)
XLA Modules:
  0.0 65.1 jit_solution(318940264036756575)
XLA Ops:
  0.0 62.8 %shard_map.91.chi_ref = f32[4,16,256]{2,1,0:T(8,128)} custom-call(s32[1,32]{1,0:T(1,128)} %bitcast.13, s32[2,32]{1,0:T(2,128)} %bitcast.11, s32[2,4,32]{2,1,0:T(4,128)} %bitcast.9, s32[4,32]{1,0:T(4,128)} %bitcast.10, bf16[1,64,256]{2,1,0:T(8,128)(2,1)} %bitcast.7, bf16[1,64,256]{2,1,0:T(8,128)(2,1)} %bitcast.8, bf16[32,64,256]{2,1,0:T(8,128)(2,1)} %blocks_hbm.1), custom_call_target="tpu_custom_call" | custom-call | tf_op jit(solution)/shard_map/pallas_call | solution.py:393
  62.8 2.3 %shard_map.92 = f32[2,64,1,16,256]{4,3,2,1,0:T(8,128)} custom-call(s32[2,4]{1,0:T(2,128)} %bitcast.12, f32[8]{0:T(128)} %constant.2.clone.cos_ref, f32[4,16,256]{2,1,0:T(8,128)} %shard_map.91.chi_ref), custom_call_target="tpu_custom_call" | custom-call | tf_op jit(solution)/shard_map/pallas_call | solution.py:440

commit v3 on v2

--- a/solution.py
+++ b/solution.py
@@ -19,8 +19,8 @@
     (-1, 3), (1, 3), (-1, 1), (0, 2), (1, 2), (-1, 2),
 ]
 HOME = [
-    (0, 0), (2, 2), (-2, 2), (2, 3), (-2, 1), (2, 1), (-2, 3), (1, 2), (-1, 2), (2, 0),
-    (-2, 0), (1, 1), (-1, 3), (1, 3), (-1, 1), (0, 2), (0, 1), (0, 3), (1, 0), (-1, 0),
+    (0, 0), (1, 0), (-1, 0), (0, 1), (0, 3), (0, 2), (1, 1), (-1, 3), (1, 3), (-1, 1), (2, 0),
+    (-2, 0), (1, 2), (-1, 2), (2, 1), (-2, 3), (2, 3), (-2, 1), (2, 2), (-2, 2),
 ]
 NA, NH = len(ALT), len(HOME)
 NPAIR = NA + NH
@@ -313,10 +313,10 @@
     chih[...] = jnp.zeros_like(chih)
     run_groups(recva, ar_sem, chia, 0, 0, NA // 4)
     to_sibling(chia, sa, sra, 0)
-    run_groups(recvh, hr_sem, chih, NA, 0, 1)
     out_ref[...] = to_chips(chia, sa, sra, za, 0)
     for d in (4, 3, 5, 2, 6, 1, 7):
         zcopy(za, zra, 0, d).start()
+    run_groups(recvh, hr_sem, chih, NA, 0, 1)
     run_groups(recvh, hr_sem, chih, NA, 1, 3)
     total = out_ref[...]
     for d in range(1, NZ):

time: 65.2 us -> 63.4 us (0.972)
  Pallas kernels: 65.1 us -> 63.2 us
    pallas_call x1, Pallas kernels: 62.8 us -> 60.9 us  [local(): pl.pallas_call(main_kernel, out_shape=jax.ShapeDtypeStruct((cells, 16, wi...]
where the time goes in v3:
time: 63.4 us; the launch traced here: 63.2 us
  Pallas kernels  63.2 us (100%)
    pallas_call x1, Pallas kernels, local(): pl.pallas_call(main_kernel, out_shape=jax.ShapeDtypeStruct((cells, 16, wi...  60.9 us
    pallas_call x1, Pallas kernels, local(): pl.pallas_call(phase_kernel, out_shape=jax.ShapeDtypeStruct(full, F32), i...  2.3 us

profile of v3, /device:TPU:1, one launch (start us, length us, event | category | flops | bytes accessed | tf_op | source)
XLA Modules:
  0.0 63.2 jit_solution(18386216369759928978)
XLA Ops:
  0.0 60.9 %shard_map.91.chi_ref = f32[4,16,256]{2,1,0:T(8,128)} custom-call(s32[1,32]{1,0:T(1,128)} %bitcast.13, s32[2,32]{1,0:T(2,128)} %bitcast.11, s32[2,4,32]{2,1,0:T(4,128)} %bitcast.9, s32[4,32]{1,0:T(4,128)} %bitcast.10, bf16[1,64,256]{2,1,0:T(8,128)(2,1)} %bitcast.7, bf16[1,64,256]{2,1,0:T(8,128)(2,1)} %bitcast.8, bf16[32,64,256]{2,1,0:T(8,128)(2,1)} %blocks_hbm.1), custom_call_target="tpu_custom_call" | custom-call | tf_op jit(solution)/shard_map/pallas_call | solution.py:393
  60.9 2.3 %shard_map.92 = f32[2,64,1,16,256]{4,3,2,1,0:T(8,128)} custom-call(s32[2,4]{1,0:T(2,128)} %bitcast.12, f32[8]{0:T(128)} %constant.2.clone.cos_ref, f32[4,16,256]{2,1,0:T(8,128)} %shard_map.91.chi_ref), custom_call_target="tpu_custom_call" | custom-call | tf_op jit(solution)/shard_map/pallas_call | solution.py:440

commit v4 on v3

--- a/solution.py
+++ b/solution.py
@@ -446,7 +446,7 @@
             pl.BlockSpec(memory_space=pltpu.VMEM),
         ],
         out_specs=pl.BlockSpec(memory_space=pl.ANY),
-        scratch_shapes=[pltpu.VMEM(full, F32), pltpu.SemaphoreType.DMA((8,))],
+        scratch_shapes=[pltpu.VMEM(full, F32), pltpu.SemaphoreType.DMA((16,))],
     )(lattice.T, table, chi)
 
 

time: 63.4 us -> 63.6 us (level)
  no operation moved by 1% of the time
where the time goes in v4:
time: 63.6 us; the launch traced here: 63.4 us
  Pallas kernels  63.4 us (100%)
    pallas_call x1, Pallas kernels, local(): pl.pallas_call(main_kernel, out_shape=jax.ShapeDtypeStruct((cells, 16, wi...  60.9 us
    pallas_call x1, Pallas kernels, local(): pl.pallas_call(phase_kernel, out_shape=jax.ShapeDtypeStruct(full, F32), i...  2.48 us

profile of v4, /device:TPU:1, one launch (start us, length us, event | category | flops | bytes accessed | tf_op | source)
XLA Modules:
  0.0 63.4 jit_solution(3946988466713182194)
XLA Ops:
  0.0 60.9 %shard_map.91.chi_ref = f32[4,16,256]{2,1,0:T(8,128)} custom-call(s32[1,32]{1,0:T(1,128)} %bitcast.13, s32[2,32]{1,0:T(2,128)} %bitcast.11, s32[2,4,32]{2,1,0:T(4,128)} %bitcast.9, s32[4,32]{1,0:T(4,128)} %bitcast.10, bf16[1,64,256]{2,1,0:T(8,128)(2,1)} %bitcast.7, bf16[1,64,256]{2,1,0:T(8,128)(2,1)} %bitcast.8, bf16[32,64,256]{2,1,0:T(8,128)(2,1)} %blocks_hbm.1), custom_call_target="tpu_custom_call" | custom-call | tf_op jit(solution)/shard_map/pallas_call | solution.py:393
  60.9 2.5 %shard_map.92 = f32[2,64,1,16,256]{4,3,2,1,0:T(8,128)} custom-call(s32[2,4]{1,0:T(2,128)} %bitcast.12, f32[8]{0:T(128)} %constant.2.clone.cos_ref, f32[4,16,256]{2,1,0:T(8,128)} %shard_map.91.chi_ref), custom_call_target="tpu_custom_call" | custom-call | tf_op jit(solution)/shard_map/pallas_call | solution.py:440
